TPU v7x, 32 devices: a whole 2x2x4 slice. The times are simulated.
32 devices in a mesh: grp: 2 (over y), seq: 8 (over z, x), head: 2 (over core).
Axes of the slice: x: 2, y: 2, z: 4, core: 2. Of those that a mesh axis runs over, the one named last changes fastest.
Arguments:
- queries: bfloat16 [2048, 32, 128], P(('grp', 'seq'), 'head'), parts along dimension 0, may hold values from -6 to 6
- new_keys: bfloat16 [2048, 4, 128], P(('grp', 'seq'), 'head'), parts along dimension 0, may hold values from -6 to 6
- incoming_values: bfloat16 [2048, 4, 128], P(('grp', 'seq'), 'head'), parts along dimension 0, may hold values from -6 to 6
- cache_pool_keys: bfloat16 [32, 128, 4, 128], P(('grp', 'seq'), None, 'head'), parts along dimension 0, may hold values from -6 to 6
- cache_pool_values: bfloat16 [32, 128, 4, 128], P(('grp', 'seq'), None, 'head'), parts along dimension 0, may hold values from -6 to 6
- prefix_block_table: int32 [8], P('grp'), parts along dimension 0, may hold values from 0 to 15, as said below
Outputs:
- attended: bfloat16 [2048, 4096], P(('grp', 'seq'), 'head'), parts along dimension 0
There are 2 independent parts, one for each index of `grp`. A program takes and returns all parts, laid end to end along the dimension named above; each array names one. Nothing has to cross between parts.
Inputs may be any that keep to these rules, and one draw needn't show every extreme that they name: `prefix_block_table`: 4 distinct pool block numbers; block number b is held at position b % 2 by index b // 2 of seq, and no two entries are held by the same index.
All inputs are finite; a program needn't handle non-finite values.
Results may differ from a plain program's by a relative error of at most 0.008.
Values may be sent and summed in bfloat16 or wider, within the bound.
No kernel may reach another device: no remote copies, remote signals or barrier semaphores. Data moves between devices by JAX's collectives and lax.ppermute only.
A program may use at most 128 MiB of HBM per device.

v0:
```python
import math
import jax
import jax.numpy as jnp
from jax import lax
from jax.sharding import PartitionSpec as P

neg_large = -1e30


def absorb(state, queries, keys, value_rows, keep, scale):
    running_max, running_total, summed = state
    scores = jnp.einsum("rkgd,skd->rkgs", queries, keys, preferred_element_type=jnp.float32) * scale
    masked = jnp.where(keep, scores, neg_large)
    top = jnp.maximum(running_max, jnp.max(masked, axis=-1))
    weights = jnp.where(keep, jnp.exp(masked - top[..., None]), 0.0)
    fade = jnp.exp(running_max - top)
    running_total = running_total * fade + jnp.sum(weights, axis=-1)
    summed = summed * fade[..., None] + jnp.einsum(
        "rkgs,skd->rkgd",
        weights.astype(jnp.bfloat16),
        value_rows,
        preferred_element_type=jnp.float32,
    )
    return (top, running_total, summed)


def sweep(state, queries, places, keys, value_rows, offset, causal, scale):
    total_keys = keys.shape[0]
    step = math.gcd(total_keys, 1024)
    turns = total_keys // step
    key_blocks = keys.reshape(turns, step, keys.shape[1], keys.shape[2])
    value_blocks = value_rows.reshape(turns, step, value_rows.shape[1], value_rows.shape[2])
    latest = jnp.max(places)

    def turn(carry, item):
        key_tile, value_tile, number = item
        opening = offset + number * step
        if causal:
            key_places = opening + jnp.arange(step, dtype=jnp.int32)
            keep = (key_places[None, :] <= places[:, None])[:, None, None, :]
            updated = lax.cond(
                opening <= latest,
                lambda held: absorb(held, queries, key_tile, value_tile, keep, scale),
                lambda held: held,
                carry,
            )
        else:
            keep = jnp.ones((1, 1, 1, step), dtype=jnp.bool_)
            updated = absorb(carry, queries, key_tile, value_tile, keep, scale)
        return (updated, None)

    result, trail = lax.scan(
        turn, state, (key_blocks, value_blocks, jnp.arange(turns, dtype=jnp.int32))
    )
    return result


def combine(left, right):
    top = jnp.maximum(left[0], right[0])
    fade_left = jnp.exp(left[0] - top)
    fade_right = jnp.exp(right[0] - top)
    return (
        top,
        left[1] * fade_left + right[1] * fade_right,
        left[2] * fade_left[..., None] + right[2] * fade_right[..., None],
    )


def finish(state):
    return (state[2] / state[1][..., None]).reshape(state[2].shape[0], -1).astype(jnp.bfloat16)


def blank_state(query_height, kv_heads, query_groups, width):
    return (
        jnp.full((query_height, kv_heads, query_groups), neg_large, jnp.float32),
        jnp.zeros((query_height, kv_heads, query_groups), jnp.float32),
        jnp.zeros((query_height, kv_heads, query_groups, width), jnp.float32),
    )


def body(
    queries, new_keys, incoming_values, cache_pool_keys, cache_pool_values, prefix_block_table
):
    query_height = queries.shape[0]
    half = query_height // 2
    kv_heads = new_keys.shape[1]
    width = queries.shape[2]
    query_groups = queries.shape[1] // kv_heads
    scale = 1.0 / math.sqrt(width)
    index = lax.axis_index("seq")
    every_keys, every_values = (
        lax.all_gather(cache_pool_keys, "seq", axis=0, tiled=True),
        lax.all_gather(cache_pool_values, "seq", axis=0, tiled=True),
    )
    gathered_prefix_keys = jnp.take(every_keys, prefix_block_table, axis=0)
    gathered_prefix_values = jnp.take(every_values, prefix_block_table, axis=0)
    gathered_prefix_keys = gathered_prefix_keys.reshape(-1, kv_heads, width)
    gathered_prefix_values = gathered_prefix_values.reshape(-1, kv_heads, width)
    grouped_queries = queries.reshape(query_height, kv_heads, query_groups, width)
    first_rows = grouped_queries[:half]
    first_places = index * query_height + jnp.arange(half, dtype=jnp.int32)
    second_rows = grouped_queries[half:]
    second_places = index * query_height + half + jnp.arange(half, dtype=jnp.int32)
    empty = blank_state(half, kv_heads, query_groups, width)
    start = jnp.int32(0)
    piece_keys = lax.all_gather(new_keys, "seq", axis=0, tiled=True)
    piece_values = lax.all_gather(incoming_values, "seq", axis=0, tiled=True)
    fresh_first = sweep(
        empty, first_rows, first_places, piece_keys, piece_values, start, True, scale
    )
    fresh_second = sweep(
        empty, second_rows, second_places, piece_keys, piece_values, start, True, scale
    )
    cached_first = sweep(
        empty,
        first_rows,
        first_places,
        gathered_prefix_keys,
        gathered_prefix_values,
        0,
        False,
        scale,
    )
    cached_second = sweep(
        empty,
        second_rows,
        second_places,
        gathered_prefix_keys,
        gathered_prefix_values,
        0,
        False,
        scale,
    )
    first_out = finish(combine(cached_first, fresh_first))
    second_out = finish(combine(cached_second, fresh_second))
    return jnp.concatenate([first_out, second_out], axis=0)


def solution(mesh):
    in_specs = (
        P(("grp", "seq"), "head", None),
        P(("grp", "seq"), "head", None),
        P(("grp", "seq"), "head", None),
        P(("grp", "seq"), None, "head", None),
        P(("grp", "seq"), None, "head", None),
        P("grp"),
    )
    out_specs = P(("grp", "seq"), "head")
    return jax.shard_map(body, mesh=mesh, in_specs=in_specs, out_specs=out_specs, check_vma=False)
```

profile of v0, /device:TPU:0, one launch (start us, length us, event | category | flops | bytes accessed | tf_op | source)
XLA Modules:
  0.0 112.6 jit_solution(26277959680551968)
XLA Ops:
  6.5 0.0 all-gather.3.cloned.1.call-start
  6.5 1.6 %copy.53 = bf16[2,128,2,128]{3,1,2,0:T(8,128)(2,1)} copy(bf16[2,128,2,128]{3,2,1,0:T(2,128)(2,1)} %param.15) | data formatting | bytes 262144 | tf_op args[3]
  8.1 0.0 all-gather.3.cloned.1.call-update
  8.1 0.0 all-gather.5.cloned.1.call-start
  8.2 1.6 %copy.56 = bf16[2,128,2,128]{3,1,2,0:T(8,128)(2,1)} copy(bf16[2,128,2,128]{3,2,1,0:T(2,128)(2,1)} %param.16) | data formatting | bytes 262144 | tf_op args[4]
  9.8 0.0 all-gather.5.cloned.1.call-update
  9.8 1.1 fusion.68
  10.9 0.1 copy.55
  10.9 0.9 copy.58
  11.8 0.9 copy.59
  12.7 0.7 add_reduce_fusion.1
  14.0 0.1 copy.61
  14.1 0.7 add_reduce_fusion
  15.5 0.1 broadcast_in_dim.112
  15.6 33.7 %all_gather.14 = bf16[1024,2,128]{2,0,1:T(8,128)(2,1)S(1)} all-gather(bf16[128,2,128]{2,0,1:T(8,128)(2,1)S(1)} %copy.58), channel_id=1, replica_groups=mesh['grp'=2,'seq'=8,'head'=2] {'seq'}, dimensions={0}, use_global_device_ids=true | all-gather | bytes 589824 | tf_op jit(solution)/shard_map/all_gather | solution.py:106
  49.3 31.7 %all_gather.15 = bf16[1024,2,128]{2,0,1:T(8,128)(2,1)S(1)} all-gather(bf16[128,2,128]{2,0,1:T(8,128)(2,1)S(1)} %copy.59), channel_id=1, replica_groups=mesh['grp'=2,'seq'=8,'head'=2] {'seq'}, dimensions={0}, use_global_device_ids=true | all-gather | bytes 589824 | tf_op jit(solution)/shard_map/all_gather | solution.py:107
  81.0 6.6 %conditional.2 = (f32[64,2,8]{0,2,1:T(8,128)}, f32[64,2,8]{0,2,1:T(8,128)S(1)}, f32[64,2,8,128]{3,0,2,1:T(8,128)S(1)}) conditional(s32[]{:T(128)} %convert_element_type.35, (f32[64,2,8]{0,2,1:T(8,128)S(1)}, f32[64,2,8]{0,2,1:T(8,128)S(1)}, f32[64,2,8,128]{3,0,2,1:T(8,128)S(1)}) %tuple.28, (s32[1024]{0:T(1024)S(1)}, s32[]{:T(128)}, ...), branch_computations={%region_2.4_spmd, %region_3.0_spmd} | conditional | flops 550832192 | bytes 15266588 | solution.py:41
  81.0 0.1 broadcast_compare_fusion
  81.1 0.9 fusion
  82.0 0.6 max.28
  82.6 2.0 %fusion.2 = f32[64,2,8]{0,2,1:T(8,128)S(1)} fusion(f32[2,1024,64,8]{1,2,3,0:T(8,128)S(1)} %get-tuple-element.203, f32[64,2,8]{0,2,1:T(8,128)} %max.28, pred[64,1024]{1,0:T(8,128)(4,1)S(1)} %broadcast_compare_fusion), kind=kLoop, calls=%fused_computation.6 | loop fusion | flops 5241856 | bytes 4268032 | tf_op jit(solution)/shard_map/while/body/eval_jaxpr/cond/branch_1_fun/reduce_sum | solution.py:17
  84.6 0.7 multiply_add_fusion
  85.3 2.2 %fusion.9 = f32[64,2,8,128]{3,0,2,1:T(8,128)S(1)} fusion(f32[2,1024,64,8]{1,2,3,0:T(8,128)S(1)} %get-tuple-element.203, f32[64,2,8]{0,2,1:T(8,128)} %max.28, pred[64,1024]{1,0:T(8,128)(4,1)S(1)} %broadcast_compare_fusion, bf16[1024,2,128]{2,0,1:T(8,128)(2,1)S(1)} %get-tuple-element.168, f32[64,2,8,128]{3,0,2,1:T(8,128)S(1)} %get-tuple-element.160, ...), kind=kOutput, calls=%fused_computation.10 | convolution fusion | flops 273940480 | bytes 5840896 | tf_op jit(solution)/shard_map/while/body/eval_jaxpr/cond/branch_1_fun/rkgs,skd->rkgd/dot_general | solution.py:18
  87.6 0.0 copy-start
  87.6 6.6 %conditional.3 = (f32[64,2,8]{0,2,1:T(8,128)}, f32[64,2,8]{0,2,1:T(8,128)S(1)}, f32[64,2,8,128]{3,0,2,1:T(8,128)S(1)}) conditional(s32[]{:T(128)} %convert_element_type.39, (f32[64,2,8]{0,2,1:T(8,128)S(1)}, f32[64,2,8]{0,2,1:T(8,128)S(1)}, f32[64,2,8,128]{3,0,2,1:T(8,128)S(1)}) %tuple.28, (s32[1024]{0:T(1024)S(1)}, s32[]{:T(128)}, ...), branch_computations={%region_9.11_spmd, %region_10.14_spmd} | conditional | flops 550832192 | bytes 15266588 | solution.py:41
  87.6 0.1 broadcast_compare_fusion.1
  87.7 0.9 fusion.18
  88.6 0.6 max.29
  89.2 2.0 %fusion.20 = f32[64,2,8]{0,2,1:T(8,128)S(1)} fusion(f32[2,1024,64,8]{1,2,3,0:T(8,128)S(1)} %get-tuple-element.205, f32[64,2,8]{0,2,1:T(8,128)} %max.29, pred[64,1024]{1,0:T(8,128)(4,1)S(1)} %broadcast_compare_fusion.1), kind=kLoop, calls=%fused_computation.25 | loop fusion | flops 5241856 | bytes 4268032 | tf_op jit(solution)/shard_map/while/body/eval_jaxpr/cond/branch_1_fun/reduce_sum | solution.py:17
  91.2 0.7 multiply_add_fusion.1
  91.9 2.2 %fusion.27 = f32[64,2,8,128]{3,0,2,1:T(8,128)S(1)} fusion(f32[2,1024,64,8]{1,2,3,0:T(8,128)S(1)} %get-tuple-element.205, f32[64,2,8]{0,2,1:T(8,128)} %max.29, pred[64,1024]{1,0:T(8,128)(4,1)S(1)} %broadcast_compare_fusion.1, bf16[1024,2,128]{2,0,1:T(8,128)(2,1)S(1)} %get-tuple-element.179, f32[64,2,8,128]{3,0,2,1:T(8,128)S(1)} %get-tuple-element.178, ...), kind=kOutput, calls=%fused_computation.29 | convolution fusion | flops 273940480 | bytes 5840896 | tf_op jit(solution)/shard_map/while/body/eval_jaxpr/cond/branch_1_fun/rkgs,skd->rkgd/dot_general | solution.py:18
  94.2 0.0 all-gather.3.cloned.1.call-done
  94.3 1.8 %gather_fusion = bf16[4,128,2,128]{3,1,2,0:T(8,128)(2,1)S(1)} fusion(bf16[16,128,2,128]{3,1,2,0:T(8,128)(2,1)} %all-gather.3.cloned.1.call-done, s32[1024]{0:T(1024)S(1)} %pad_clamp_fusion), kind=kCustom, calls=%fused_computation.clone | custom fusion | bytes 524304 | tf_op jit(solution)/shard_map/jit(_take)/gather | solution.py:95
  96.1 0.7 all-gather.5.cloned.1.call-done
  96.8 1.8 %gather_fusion.1 = bf16[4,128,2,128]{3,1,2,0:T(8,128)(2,1)S(1)} fusion(bf16[16,128,2,128]{3,1,2,0:T(8,128)(2,1)} %all-gather.5.cloned.1.call-done, s32[1024]{0:T(1024)S(1)} %pad_clamp_fusion), kind=kCustom, calls=%fused_computation.1.clone | custom fusion | bytes 524304 | tf_op jit(solution)/shard_map/jit(_take)/gather | solution.py:96
  98.7 0.1 broadcast_select_fusion.1
  98.8 0.5 bitcast_reduce_fusion.1
  99.3 0.5 bitcast_reduce_fusion
  99.9 0.6 fusion.38
  100.5 0.7 multiply_add_fusion.3
  101.2 1.0 fusion.51
  102.2 0.2 copy.60
  102.4 0.6 fusion.40
  103.0 0.7 multiply_add_fusion.2
  103.7 1.0 fusion.50
  104.7 0.2 copy.62
  104.9 0.1 copy_bitcast_fusion
  105.0 0.8 pad_maximum_fusion
  (16 shorter events, 0.1 us)
Async XLA Ops:
  6.5 87.7 %all-gather.3.cloned.1.call-start = ((), (), s32[]{:S(2)}) async-start(), calls=%async_computation | async-start | bytes 1179648 | tf_op jit(solution)/shard_map/all_gather | solution.py:92
  8.1 88.7 %all-gather.5.cloned.1.call-start = ((), (), s32[]{:S(2)}) async-start(), calls=%async_computation.1 | async-start | bytes 1179648 | tf_op jit(solution)/shard_map/all_gather | solution.py:93
  87.6 6.6 %copy-start = (s32[4]{0:T(128)S(1)}, s32[4]{0:T(128)}, u32[]{:S(2)}) copy-start(s32[4]{0:T(128)} %param.17) | copy-start | bytes 52
Sparse Core Ops, SparseCore 0:
  9.5 45.5 all-gather.2
  57.1 39.6 all-gather.4
where the time goes:
time: 113 us
  blocking collectives  65.4 us (58%)
  between operations  15 us (13%)
  other arithmetic  11.9 us (11%)
  local copies, waits for them, and re-layouts  10.3 us (9%)
  matrix products  9.21 us (8%)
    all_gather x1, blocking collectives, body(): piece_keys = lax.all_gather(new_keys, 'seq', axis=0, tiled=True)  33.7 us
    all_gather x1, blocking collectives, body(): piece_values = lax.all_gather(incoming_values, 'seq', axis=0, tiled=True)  31.7 us
    dot_general x4, matrix products, absorb(): jnp.einsum('rkgs,skd->rkgd', weights.astype(jnp.bfloat16), value_rows, pr...  6.43 us
    reduce_sum x4, other arithmetic, absorb(): running_total = running_total * fade + jnp.sum(weights, axis=-1)  5.22 us
    unnamed x6, local copies, waits for them, and re-layouts  4.86 us
    dot_general x4, matrix products, absorb(): jnp.einsum('rkgd,skd->rkgs', queries, keys, preferred_element_type=jnp.fl...  2.78 us
  transfers between devices with their start and end apart: 2, of which 1 were waited for; matrix products, arithmetic and copies ran while one was open for 19% of the time, Pallas kernels for 0%

commit v1 on v0

--- a/solution.py
+++ b/solution.py
@@ -103,8 +103,13 @@
     second_places = index * query_height + half + jnp.arange(half, dtype=jnp.int32)
     empty = blank_state(half, kv_heads, query_groups, width)
     start = jnp.int32(0)
-    piece_keys = lax.all_gather(new_keys, "seq", axis=0, tiled=True)
-    piece_values = lax.all_gather(incoming_values, "seq", axis=0, tiled=True)
+    piece_keys, piece_values = jnp.split(
+        lax.all_gather(
+            jnp.concatenate([new_keys, incoming_values], axis=1), "seq", axis=0, tiled=True
+        ),
+        [new_keys.shape[1]],
+        axis=1,
+    )
     fresh_first = sweep(
         empty, first_rows, first_places, piece_keys, piece_values, start, True, scale
     )

time: 113 us -> 165 us (1.46)
  waiting for transfers between devices: 0.8 us -> 111 us
  blocking collectives: 65.4 us -> 0 us
  local copies, waits for them, and re-layouts: 10.3 us -> 14.5 us
  other arithmetic: 11.9 us -> 13.8 us
    all_gather x2 -> x0, blocking collectives: 65.4 us -> none  [the longest x1 33.7 us: body(): piece_keys = lax.all_gather(new_keys, 'seq', axis=0, tiled=True)]
    all_gather x1, waiting for transfers between devices: 0.75 us -> 39.3 us  [body(): lax.all_gather(cache_pool_values, 'seq', axis=0, tiled=True)]
    all_gather x0 -> x1, waiting for transfers between devices: none -> 37.4 us  [body(): lax.all_gather(jnp.concatenate([new_keys, incoming_values], axis=1), 'seq...]
    all_gather x1, waiting for transfers between devices: 0.02 us -> 34.3 us  [body(): lax.all_gather(cache_pool_keys, 'seq', axis=0, tiled=True)]
    split x0 -> x1, local copies, waits for them, and re-layouts: none -> 2.07 us  [body(): jnp.split(lax.all_gather(jnp.concatenate([new_keys, incoming_values], axi...]
    unnamed x6 -> x10, local copies, waits for them, and re-layouts: 4.86 us -> 4.88 us
  transfers between devices with their start and end apart: 2 -> 3, of which waited for: 1 -> 3; matrix products, arithmetic and copies ran while one was open for 19% -> 9% of each run, Pallas kernels for 0% -> 0%
where the time goes in v1:
time: 165 us
  waiting for transfers between devices  111 us (67%)
  between operations  14.6 us (9%)
  local copies, waits for them, and re-layouts  14.5 us (9%)
  other arithmetic  13.8 us (8%)
  matrix products  10.5 us (6%)
    all_gather x1, waiting for transfers between devices, body(): lax.all_gather(cache_pool_values, 'seq', axis=0, tiled=True)  39.3 us
    all_gather x1, waiting for transfers between devices, body(): lax.all_gather(jnp.concatenate([new_keys, incoming_values], axis=1), 'seq...  37.4 us
    all_gather x1, waiting for transfers between devices, body(): lax.all_gather(cache_pool_keys, 'seq', axis=0, tiled=True)  34.3 us
    dot_general x4, matrix products, absorb(): jnp.einsum('rkgs,skd->rkgd', weights.astype(jnp.bfloat16), value_rows, pr...  7.74 us
    reduce_sum x4, other arithmetic, absorb(): running_total = running_total * fade + jnp.sum(weights, axis=-1)  5.19 us
    unnamed x10, local copies, waits for them, and re-layouts  4.88 us
  transfers between devices with their start and end apart: 3, of which 3 were waited for; matrix products, arithmetic and copies ran while one was open for 9% of the time, Pallas kernels for 0%

profile of v1, /device:TPU:0, one launch (start us, length us, event | category | flops | bytes accessed | tf_op | source)
XLA Modules:
  0.0 164.6 jit_solution(16174851822935580780)
XLA Ops:
  6.5 1.6 copy.53
  8.2 1.6 copy.56
  9.8 0.0 all-gather.8.cloned.1.call-start
  9.8 0.9 copy.58
  10.7 0.9 copy.59
  11.6 0.7 pad_maximum_fusion.1
  12.2 1.1 fusion.69
  13.3 0.1 copy.55
  13.4 0.6 add_reduce_fusion.1
  14.7 0.1 copy.61
  14.8 0.6 add_reduce_fusion
  16.1 0.8 broadcast_in_dim.112
  16.9 0.7 compare_select_fusion
  17.6 0.7 compare_and_fusion
  18.2 34.3 %all-gather.4.cloned.1.call-done = bf16[16,128,2,128]{3,1,2,0:T(8,128)(2,1)} async-done(((bf16[2,128,2,128]{3,1,2,0:T(8,128)(2,1)}), bf16[16,128,2,128]{3,1,2,0:T(8,128)(2,1)}) %all-gather.4.cloned.1.call-update) | async-done | bytes 1048592 | tf_op jit(solution)/shard_map/all_gather | solution.py:92
  52.5 1.8 %gather_fusion = bf16[4,128,2,128]{3,1,2,0:T(8,128)(2,1)S(1)} fusion(bf16[16,128,2,128]{3,1,2,0:T(8,128)(2,1)} %all-gather.4.cloned.1.call-done, s32[1024]{0:T(1024)S(1)} %pad_clamp_fusion), kind=kCustom, calls=%fused_computation.clone | custom fusion | bytes 524304 | tf_op jit(solution)/shard_map/jit(_take)/gather | solution.py:95
  54.3 39.3 %all-gather.6.cloned.1.call-done = bf16[16,128,2,128]{3,1,2,0:T(8,128)(2,1)} async-done(((bf16[2,128,2,128]{3,1,2,0:T(8,128)(2,1)}), bf16[16,128,2,128]{3,1,2,0:T(8,128)(2,1)}) %all-gather.6.cloned.1.call-update) | async-done | bytes 1048592 | tf_op jit(solution)/shard_map/all_gather | solution.py:93
  93.6 1.8 %gather_fusion.1 = bf16[4,128,2,128]{3,1,2,0:T(8,128)(2,1)S(1)} fusion(bf16[16,128,2,128]{3,1,2,0:T(8,128)(2,1)} %all-gather.6.cloned.1.call-done, s32[1024]{0:T(1024)S(1)} %pad_clamp_fusion), kind=kCustom, calls=%fused_computation.1.clone | custom fusion | bytes 524304 | tf_op jit(solution)/shard_map/jit(_take)/gather | solution.py:96
  95.5 0.1 broadcast_select_fusion.1
  95.6 0.7 copy.57
  96.3 0.5 bitcast_reduce_fusion.1
  96.8 0.6 fusion.38
  97.4 37.4 %all-gather.8.cloned.1.call-done = bf16[1024,4,128]{2,0,1:T(8,128)(2,1)} async-done(((bf16[128,4,128]{2,0,1:T(8,128)(2,1)}), bf16[1024,4,128]{2,0,1:T(8,128)(2,1)}) %all-gather.8.cloned.1.call-update) | async-done | bytes 1048592 | tf_op jit(solution)/shard_map/all_gather | solution.py:107
  134.8 2.1 %fusion.68 = (bf16[1024,2,128]{2,0,1:T(8,128)(2,1)}, bf16[1024,2,128]{2,0,1:T(8,128)(2,1)S(1)}) fusion(bf16[1024,4,128]{2,0,1:T(8,128)(2,1)} %all-gather.8.cloned.1.call-done), kind=kLoop, calls=%fused_computation.93 | loop fusion | bytes 2097152 | tf_op jit(solution)/shard_map/split | solution.py:106
  136.9 6.7 %conditional.2 = (f32[64,2,8]{0,2,1:T(8,128)}, f32[64,2,8]{0,2,1:T(8,128)S(1)}, f32[64,2,8,128]{3,0,2,1:T(8,128)S(1)}) conditional(s32[]{:T(128)} %convert_element_type.35, (f32[64,2,8]{0,2,1:T(8,128)S(1)}, f32[64,2,8]{0,2,1:T(8,128)S(1)}, f32[64,2,8,128]{3,0,2,1:T(8,128)}) %tuple.28, (s32[1024]{0:T(1024)S(1)}, s32[]{:T(128)}, s32[64,1]{0,1:T(1,128)S(1)}, ...), branch_computations={%region_2.4_spmd, %region_3.0_spmd} | conditional | flops 550832192 | bytes 17363768 | solution.py:41
  136.9 0.1 broadcast_compare_fusion
  137.0 0.9 fusion
  137.9 0.6 max.28
  138.5 2.0 %fusion.2 = f32[64,2,8]{0,2,1:T(8,128)S(1)} fusion(f32[2,1024,64,8]{1,2,3,0:T(8,128)S(1)} %get-tuple-element.203, f32[64,2,8]{0,2,1:T(8,128)} %max.28, pred[64,1024]{1,0:T(8,128)(4,1)S(1)} %broadcast_compare_fusion), kind=kLoop, calls=%fused_computation.6 | loop fusion | flops 5241856 | bytes 4268032 | tf_op jit(solution)/shard_map/while/body/eval_jaxpr/cond/branch_1_fun/reduce_sum | solution.py:17
  140.5 0.7 multiply_add_fusion
  141.2 2.4 %fusion.9 = f32[64,2,8,128]{3,0,2,1:T(8,128)S(1)} fusion(f32[2,1024,64,8]{1,2,3,0:T(8,128)S(1)} %get-tuple-element.203, f32[64,2,8]{0,2,1:T(8,128)} %max.28, pred[64,1024]{1,0:T(8,128)(4,1)S(1)} %broadcast_compare_fusion, bf16[1024,2,128]{2,0,1:T(8,128)(2,1)} %get-tuple-element.168, f32[64,2,8,128]{3,0,2,1:T(8,128)S(1)} %copy-done.1, ...), kind=kOutput, calls=%fused_computation.10 | convolution fusion | flops 273940480 | bytes 5840896 | tf_op jit(solution)/shard_map/while/body/eval_jaxpr/cond/branch_1_fun/rkgs,skd->rkgd/dot_general | solution.py:18
  143.7 0.8 multiply_add_fusion.3
  144.4 2.0 %fusion.51 = bf16[64,2,8,128]{3,0,2,1:T(8,128)(2,1)S(1)} fusion(bf16[512,2,128,1]{2,0,3,1:T(8,128)(2,1)} %bitcast.146, f32[2,512,64,8]{1,2,3,0:T(8,128)S(1)} %get-tuple-element.217, f32[64,2,8]{0,2,1:T(8,128)S(1)} %broadcast_maximum_fusion.1, f32[64,2,8,128]{3,0,2,1:T(8,128)S(1)} %get-tuple-element.187, f32[64,2,8]{0,2,1:T(8,128)S(1)} %get-tuple-element.196, ...), kind=kOutput, calls=%fused_computation.61 | convolution fusion | flops 136577024 | bytes 3166208 | tf_op jit(solution)/shard_map/while/body/eval_jaxpr/rkgs,skd->rkgd/dot_general | solution.py:18
  146.4 0.9 copy.60
  147.3 0.5 bitcast_reduce_fusion
  147.8 6.8 %conditional.3 = (f32[64,2,8]{0,2,1:T(8,128)}, f32[64,2,8]{0,2,1:T(8,128)S(1)}, f32[64,2,8,128]{3,0,2,1:T(8,128)S(1)}) conditional(s32[]{:T(128)} %convert_element_type.39, (f32[64,2,8]{0,2,1:T(8,128)S(1)}, f32[64,2,8]{0,2,1:T(8,128)S(1)}, f32[64,2,8,128]{3,0,2,1:T(8,128)S(1)}) %tuple.59, (s32[1024]{0:T(1024)S(1)}, s32[]{:T(128)}, ...), branch_computations={%region_9.11_spmd, %region_10.14_spmd} | conditional | flops 550832192 | bytes 15266588 | solution.py:41
  147.9 0.1 broadcast_compare_fusion.1
  148.0 0.9 fusion.18
  148.9 0.6 max.29
  149.5 2.0 %fusion.20 = f32[64,2,8]{0,2,1:T(8,128)S(1)} fusion(f32[2,1024,64,8]{1,2,3,0:T(8,128)S(1)} %get-tuple-element.205, f32[64,2,8]{0,2,1:T(8,128)} %max.29, pred[64,1024]{1,0:T(8,128)(4,1)S(1)} %broadcast_compare_fusion.1), kind=kLoop, calls=%fused_computation.25 | loop fusion | flops 5241856 | bytes 4268032 | tf_op jit(solution)/shard_map/while/body/eval_jaxpr/cond/branch_1_fun/reduce_sum | solution.py:17
  151.5 0.7 multiply_add_fusion.1
  152.2 2.4 %fusion.27 = f32[64,2,8,128]{3,0,2,1:T(8,128)S(1)} fusion(f32[2,1024,64,8]{1,2,3,0:T(8,128)S(1)} %get-tuple-element.205, f32[64,2,8]{0,2,1:T(8,128)} %max.29, pred[64,1024]{1,0:T(8,128)(4,1)S(1)} %broadcast_compare_fusion.1, bf16[1024,2,128]{2,0,1:T(8,128)(2,1)} %get-tuple-element.179, f32[64,2,8,128]{3,0,2,1:T(8,128)S(1)} %get-tuple-element.178, ...), kind=kOutput, calls=%fused_computation.29 | convolution fusion | flops 273940480 | bytes 5840896 | tf_op jit(solution)/shard_map/while/body/eval_jaxpr/cond/branch_1_fun/rkgs,skd->rkgd/dot_general | solution.py:18
  154.6 0.6 fusion.40
  155.2 0.7 multiply_add_fusion.2
  155.9 1.0 fusion.50
  156.9 0.2 copy.62
  157.1 0.1 copy_bitcast_fusion
  157.2 0.8 pad_maximum_fusion
  (25 shorter events, 0.2 us)
Async XLA Ops:
  6.5 46.0 %all-gather.4.cloned.1.call-start = ((), (), s32[]{:S(2)}) async-start(), calls=%async_computation | async-start | bytes 1179648 | tf_op jit(solution)/shard_map/all_gather | solution.py:92
  8.1 85.5 %all-gather.6.cloned.1.call-start = ((), (), s32[]{:S(2)}) async-start(), calls=%async_computation.1 | async-start | bytes 1179648 | tf_op jit(solution)/shard_map/all_gather | solution.py:93
  9.8 125.0 %all-gather.8.cloned.1.call-start = ((), (), s32[]{:S(2)}) async-start(), calls=%async_computation.2 | async-start | bytes 1179648 | tf_op jit(solution)/shard_map/all_gather | solution.py:107
  137.0 4.2 %copy-start.1 = (f32[64,2,8,128]{3,0,2,1:T(8,128)S(1)}, f32[64,2,8,128]{3,0,2,1:T(8,128)}, u32[]{:S(2)}) copy-start(f32[64,2,8,128]{3,0,2,1:T(8,128)} %get-tuple-element.160) | copy-start | bytes 1572868 | tf_op jit(solution)/shard_map/while/body/eval_jaxpr/cond
  143.6 4.2 %copy-start = (f32[64,2,8,128]{3,0,2,1:T(8,128)S(1)}, f32[64,2,8,128]{3,0,2,1:T(8,128)}, u32[]{:S(2)}) copy-start(f32[64,2,8,128]{3,0,2,1:T(8,128)} %broadcast_in_dim.112) | copy-start | bytes 1572868
  147.8 8.1 %copy-start.3 = (bf16[4,128,2,128]{3,1,0,2:T(8,128)(2,1)S(1)}, bf16[4,128,2,128]{3,1,0,2:T(8,128)(2,1)}, u32[]{:S(2)}) copy-start(bf16[4,128,2,128]{3,1,0,2:T(8,128)(2,1)} %copy.57) | copy-start | bytes 786436
  154.6 2.5 %copy-start.2 = (bf16[64,2,8,128]{3,2,1,0:T(8,128)(2,1)S(1)}, bf16[64,2,8,128]{3,2,1,0:T(8,128)(2,1)}, u32[]{:S(2)}) copy-start(bf16[64,2,8,128]{3,2,1,0:T(8,128)(2,1)} %copy.60) | copy-start | bytes 786436
Sparse Core Ops, SparseCore 0:
  9.5 42.9 all-gather.3
  54.6 38.9 all-gather.5
  95.8 38.9 all-gather.7
